TPU v7x, 32 devices: a whole 2x2x4 slice. The times are simulated.
32 devices in a mesh: groups: 2 (over y), ctx: 4 (over z), tp: 2 (over x), sub: 2 (over core).
Axes of the slice: x: 2, y: 2, z: 4, core: 2. Of those that a mesh axis runs over, the one named last changes fastest.
Arguments:
- x_input: bfloat16 [4096, 8192], P(('groups', 'ctx', 'sub'), 'tp'), parts along dimension 0, may hold values from -48 to 48
- gate_input: bfloat16 [4096, 8192], P(('groups', 'ctx', 'sub'), 'tp'), parts along dimension 0, may hold values from -6 to 6
- state_proj: bfloat16 [4096, 8, 2, 128], P(('groups', 'ctx', 'sub'), 'tp'), parts along dimension 0, may hold values from -2.5 to 2.5
- mix_weight: bfloat16 [4, 8192], P(None, 'tp'), may hold values from -3 to 3
- mix_bias: float32 [8192], P('tp'), may hold values from -3 to 3
- state_weight: bfloat16 [4, 8, 2, 128], P(None, 'tp'), may hold values from -3 to 3
- state_bias: float32 [8, 2, 128], P('tp'), may hold values from -2.5 to 2.5
- step_raw: float32 [4096, 128], P(('groups', 'ctx', 'sub'), 'tp'), parts along dimension 0, may hold values from -4.5 to 50
- decay_log: float32 [128], P('tp'), may hold values from -5.3 to 0.41
- skip_gain: float32 [128], P('tp'), may hold values from 0.5 to 1.5
- norm_gain: float32 [8192], P('tp'), may hold values from 0.5 to 1.5
- out_weight: bfloat16 [8192, 4096], P(('tp', 'sub')), may hold values from -0.0625 to 0.0625
- doc_lengths: int32 [16], P('groups'), parts along dimension 0, may hold values from 1 to 1024, 2048 in all
Outputs:
- output: bfloat16 [4096, 4096], P(('groups', 'ctx', 'sub'), 'tp'), parts along dimension 0
There are 2 independent parts, one for each index of `groups`. A program takes and returns all parts, laid end to end along the dimension named above; an argument that names none is the same for every part. Nothing has to cross between parts.
Inputs may be any that keep to these rules, and one draw needn't show every extreme that they name: `doc_lengths`: documents lie end to end from position 0 in the given order; the largest has exactly 1024 positions.
All inputs are finite; a program needn't handle non-finite values.
Results may differ from a plain program's by a relative error of at most 0.0095.
Values may be sent and summed in bfloat16 or wider, within the bound.
No kernel may reach another device: no remote copies, remote signals or barrier semaphores. Data moves between devices by JAX's collectives and lax.ppermute only.
A program may use at most 192 MiB of HBM per device.

v0:
```python
import functools

import jax
import jax.numpy as jnp
from jax import lax
from jax.experimental import pallas as pl
from jax.experimental.pallas import tpu as pltpu
from jax.sharding import PartitionSpec as P

HEADS = 128
GROUPS = 8
CHUNK = 128
EPSILON = 1e-05
LOG2E = 1.4426950408889634
MASKED = -1e30
F32 = jnp.float32
BF16 = jnp.bfloat16


def shifted(shard, axis, by):
    peers = lax.axis_size(axis)
    pairs = [(i, i + by) for i in range(peers) if 0 <= i + by < peers]
    return lax.ppermute(shard, axis, pairs)


def swapped(shard, axis):
    return lax.ppermute(shard, axis, [(i, i ^ 1) for i in range(lax.axis_size(axis))])


def doc_start(positions, docs_ref):
    start = jnp.zeros_like(positions)
    total = jnp.int32(0)
    for doc in range(docs_ref.shape[0]):
        start = jnp.where(positions >= total, total, start)
        total = total + docs_ref[doc]
    return start


def rows_of(count, first):
    return first + lax.broadcasted_iota(jnp.int32, (count, 1), 0)


def split2(value):
    high = value.astype(BF16)
    return high, (value - high.astype(F32)).astype(BF16)


def split3(value):
    high = value.astype(BF16)
    rest = value - high.astype(F32)
    mid = rest.astype(BF16)
    return high, mid, (rest - mid.astype(F32)).astype(BF16)


def mm(a, b):
    return jnp.dot(a, b, preferred_element_type=F32)


def contract_rows(a, b):
    return lax.dot_general(a, b, (((0,), (0,)), ((), ())), preferred_element_type=F32)


def contract_lanes(a, b):
    return lax.dot_general(a, b, (((1,), (1,)), ((), ())), preferred_element_type=F32)


def silu(value):
    half = 0.5 * value
    return half + half * jnp.tanh(half)


def head_lanes(heads, head_width, lanes, first_lane):
    head = lax.broadcasted_iota(jnp.int32, (heads, lanes), 0)
    lane = first_lane + lax.broadcasted_iota(jnp.int32, (heads, lanes), 1)
    low = head * head_width
    return jnp.where((lane >= low) & (lane < low + head_width), 1.0, 0.0).astype(BF16)


def conv_kernel(meta, docs, x, x_rim, w, bias, s, s_rim, sw, sbias, out, shift, rim_shift, *, taps):
    step, last = pl.program_id(0), pl.num_programs(0) - 1
    count = x.shape[0]
    rims = x_rim.shape[0]

    @pl.when(step == 0)
    def _():
        start = doc_start(rows_of(count, meta[0]), docs) - meta[0]
        row = lax.broadcasted_iota(jnp.int32, (count, count), 0)
        col = lax.broadcasted_iota(jnp.int32, (count, count), 1)
        rim_row = lax.broadcasted_iota(jnp.int32, (rims, rims), 0)
        rim_col = lax.broadcasted_iota(jnp.int32, (rims, rims), 1) - rims
        for back in range(1, taps):
            hit = (col == row - back) & (col >= start)
            shift[back - 1] = jnp.where(hit, 1.0, 0.0).astype(BF16)
            rim_hit = (rim_col == rim_row - back) & (rim_col >= start[:rims])
            rim_shift[back - 1] = jnp.where(rim_hit, 1.0, 0.0).astype(BF16)

    def mix(x_part, rim_part, w_part, bias_part):
        value = x_part[...]
        rim = rim_part[...]
        weight = w_part[...].astype(F32)
        summed = bias_part[...] + value.astype(F32) * weight[taps - 1 : taps]
        top = jnp.zeros((rims, value.shape[1]), F32)
        for back in range(1, taps):
            row = weight[taps - 1 - back : taps - back]
            summed = summed + mm(shift[back - 1], value) * row
            top = top + mm(rim_shift[back - 1], rim) * row
        out[:rims, :] = silu(summed[:rims] + top).astype(BF16)
        out[rims:, :] = silu(summed[rims:]).astype(BF16)

    @pl.when(step < last)
    def _():
        mix(x, x_rim, w, bias)

    @pl.when(step == last)
    def _():
        mix(s, s_rim, sw, sbias)


def conv_half(meta, docs, x, x_rim, w, bias, s, s_rim, sw, sbias, width, block):
    count = x.shape[0]
    taps = w.shape[0]
    rims = x_rim.shape[0]
    steps = width // block
    x_at = lambda i, m, d: (0, m[1] * steps + jnp.minimum(i, steps - 1))
    s_at = lambda i, m, d: (0, m[2])
    specs = []
    for at in (x_at, s_at):
        for rows in (count, rims, taps, 1):
            specs.append(pl.BlockSpec((rows, block), at))
    return pl.pallas_call(
        functools.partial(conv_kernel, taps=taps),
        grid_spec=pltpu.PrefetchScalarGridSpec(
            num_scalar_prefetch=2,
            grid=(steps + 1,),
            in_specs=specs,
            out_specs=pl.BlockSpec((count, block), lambda i, m, d: (0, i)),
            scratch_shapes=[
                pltpu.VMEM((taps - 1, count, count), BF16),
                pltpu.VMEM((taps - 1, rims, rims), BF16),
            ],
        ),
        out_shape=jax.ShapeDtypeStruct((count, width + block), BF16),
        compiler_params=pltpu.CompilerParams(vmem_limit_bytes=32 << 20),
        cost_estimate=pl.CostEstimate(
            flops=8 * count * width, bytes_accessed=4 * count * (width + block), transcendentals=count * width
        ),
        name="conv",
    )(meta, docs, x, x_rim, w, bias, s, s_rim, sw, sbias)


def state_kernel(
    meta, docs, own, got, own_bc, got_bc, own_raw, got_raw, rate,
    x_out, bc_out, s_out, d_out, cum_out, dlt_out, raw, weight,
    *, head_width, group_width, state_width,
):
    step = pl.program_id(0)
    half = own.shape[0]
    count = 2 * half
    heads = raw.shape[1]
    width = own.shape[1]
    own_at = pl.ds(pl.multiple_of(meta[0] * half, half), half)
    got_at = pl.ds(pl.multiple_of((1 - meta[0]) * half, half), half)
    first = meta[1]
    last_start = doc_start(first + count - 1, docs)

    @pl.when(step == 0)
    def _():
        bc_out[own_at, :] = own_bc[...]
        bc_out[got_at, :] = got_bc[...]
        raw[own_at, :] = own_raw[...]
        raw[got_at, :] = got_raw[...]
        value = raw[...]
        size = jnp.maximum(value, 0.0) + jnp.log(1.0 + jnp.exp(-jnp.abs(value)))
        decay = (-LOG2E * jnp.exp(rate[...])) * size
        row = lax.broadcasted_iota(jnp.int32, (count, count), 0)
        col = lax.broadcasted_iota(jnp.int32, (count, count), 1)
        below = jnp.where(col <= row, 1.0, 0.0).astype(BF16)
        high, mid, low = split3(decay)
        cum = mm(below, high) + (mm(below, mid) + mm(below, low))
        cum_out[...] = cum
        dlt_out[...] = (cum - jnp.log2(size)).T
        end = cum[count - 1 :]
        tail = jnp.where(rows_of(count, first) >= last_start, size * jnp.exp2(end - cum), 0.0)
        high, low = split2(tail)
        weight[0] = high
        weight[1] = low

    x_out[own_at, :] = own[...]
    x_out[got_at, :] = got[...]
    spread = head_lanes(heads, head_width, width, step * width)
    group = (step * width) // group_width
    b = bc_out[:, pl.ds(pl.multiple_of(group * 2 * state_width, state_width), state_width)]
    tails = mm(weight[0], spread) + mm(weight[1], spread)
    weighted = (x_out[...].astype(F32) * tails).astype(BF16)
    s_out[...] = contract_rows(b, weighted).astype(BF16)
    kept = jnp.exp2(jnp.broadcast_to(cum_out[count - 1 :, :], (8, heads)))
    high, mid, low = split3(jnp.where(last_start < first, kept, 0.0))
    d_out[...] = mm(high, spread) + (mm(mid, spread) + mm(low, spread))


def intra_kernel(
    meta, docs, x, bc, cum, dlt, gate_own, gate_got, skip,
    a_out, f_out, state, base, spread, reach, into, tail,
    *, head_width, group_heads, state_width,
):
    step = pl.program_id(0)
    count, width = x.shape
    heads = cum.shape[1]
    first = meta[1] + step * count

    @pl.when(step == 0)
    def _():
        state[...] = jnp.zeros_like(state)
        base[...] = jnp.zeros_like(base)
        spread[...] = head_lanes(heads, head_width, width, 0)

    starts = doc_start(rows_of(count, first), docs)
    last_start = doc_start(first + count - 1, docs)
    here = cum[...]
    before = base[:1, :]
    end = here[count - 1 :]
    lanes = spread[...]

    def spread_over(value):
        high, low = split2(value)
        return mm(high, lanes) + mm(low, lanes)

    reach[...] = spread_over(jnp.where(starts < first, jnp.exp2(here - before), 0.0))
    into[...] = spread_over(jnp.where(starts < meta[1], jnp.exp2(here), 0.0))
    to_end = jnp.exp2(end - dlt[...].T)
    tail[...] = spread_over(jnp.where(rows_of(count, first) >= last_start, to_end, 0.0))
    kept = jnp.broadcast_to(jnp.where(last_start < first, jnp.exp2(end - before), 0.0), (8, heads))
    high, mid, low = split3(kept)
    kept = (mm(high, lanes) + (mm(mid, lanes) + mm(low, lanes)))[:1]
    row = lax.broadcasted_iota(jnp.int32, (count, count), 0)
    col = lax.broadcasted_iota(jnp.int32, (count, count), 1)
    mask = jnp.where((col <= row) & (col >= starts - first), 0.0, MASKED)
    is_own = (step * count) // (count * (pl.num_programs(0) // 2)) == meta[0]
    low_lanes = lax.broadcasted_iota(jnp.int32, (count, 2 * head_width), 1) < head_width
    zero = jnp.zeros((count, 2 * head_width), BF16)
    for group in range(heads // group_heads):
        b = bc[:, group * 2 * state_width : (group * 2 + 1) * state_width]
        c = bc[:, (group * 2 + 1) * state_width : (group * 2 + 2) * state_width]
        scores = contract_lanes(c, b)
        for head in range(group * group_heads, (group + 1) * group_heads, 2):
            at = slice(head * head_width, (head + 2) * head_width)
            pair = []
            for k in (head, head + 1):
                exponent = (here[:, k : k + 1] - dlt[k : k + 1, :]) + mask
                pair.append((jnp.exp2(exponent) * scores).astype(BF16))
            value = x[:, at]
            stacked = jnp.concatenate([jnp.where(low_lanes, value, zero), jnp.where(low_lanes, zero, value)], axis=0)
            within = mm(jnp.concatenate(pair, axis=1), stacked)
            old = state[:, at]
            carried = mm(c, old.astype(BF16)) * reach[:, at]
            x_part = value.astype(F32)
            y = within + carried + x_part * skip[:, at]
            gate = silu(jnp.where(is_own, gate_own[:, at], gate_got[:, at]).astype(F32))
            a_out[:, at] = y * gate
            f_out[:, at] = gate * into[:, at]
            fresh = contract_rows(b, (x_part * tail[:, at]).astype(BF16))
            state[:, at] = old * kept[:, at] + fresh
    base[...] = jnp.broadcast_to(end, base.shape)


def project_kernel(
    meta, a, f, bc, incoming, gain, squares, w, hidden, send, keep,
    *, row_steps, group_width, state_width, divisor,
):
    step = pl.program_id(0)
    count = a.shape[0]
    width = a.shape[1]
    half = send.shape[0]

    @pl.when(step < row_steps)
    def _():
        at = pl.ds(pl.multiple_of(step * count, count), count)
        for group in range(width // group_width):
            lanes = slice(group * group_width, (group + 1) * group_width)
            c = bc[:, (group * 2 + 1) * state_width : (group * 2 + 2) * state_width]
            gated = a[:, lanes] + mm(c, incoming[:, lanes]) * f[:, lanes]
            if squares is None:
                total = jnp.sum(gated * gated, axis=1, keepdims=True)
            else:
                total = squares[...]
            scale = lax.rsqrt(total / divisor + EPSILON)
            hidden[at, lanes] = (gated * scale * gain[:, lanes]).astype(BF16)

    @pl.when(step >= row_steps)
    def _():
        there = pl.ds(pl.multiple_of((1 - meta[0]) * half, half), half)
        here = pl.ds(pl.multiple_of(meta[0] * half, half), half)
        send[...] = mm(hidden[there, :], w[...]).astype(BF16)
        keep[...] = mm(hidden[here, :], w[...])


def product_kernel(meta, hidden, w, send, keep):
    half = send.shape[0]
    there = pl.ds(pl.multiple_of((1 - meta[0]) * half, half), half)
    here = pl.ds(pl.multiple_of(meta[0] * half, half), half)
    send[...] = mm(hidden[there, :], w[...]).astype(BF16)
    keep[...] = mm(hidden[here, :], w[...])


def padded_rim(shard, rims):
    return jnp.concatenate([jnp.zeros((rims - shard.shape[0],) + shard.shape[1:], shard.dtype), shard])


def local(
    x_input, gate_input, state_proj, mix_weight, mix_bias, state_weight, state_bias,
    step_raw, decay_log, skip_gain, norm_gain, out_weight, doc_lengths,
):
    half, channels = x_input.shape
    all_heads = step_raw.shape[1]
    groups, _, state_width = state_proj.shape[1:]
    taps = mix_weight.shape[0]
    features = out_weight.shape[1]
    head_width = channels // all_heads
    heads = all_heads // 2
    width = channels // 2
    count = 2 * half
    whole_groups = groups % 2 == 0
    my_groups = groups // 2 if whole_groups else groups
    group_heads = heads // my_groups
    group_width = group_heads * head_width
    block = my_groups * 2 * state_width
    sub = lax.axis_index("sub").astype(jnp.int32)
    ctx = lax.axis_index("ctx").astype(jnp.int32)
    tp = lax.axis_index("tp").astype(jnp.int32)
    tp_size = lax.axis_size("tp")
    ctx_size = lax.axis_size("ctx")
    block_first = ctx * count
    docs = doc_lengths.astype(jnp.int32)
    zero = jnp.int32(0)

    s_input = state_proj.reshape(half, groups * 2 * state_width)
    s_weight = state_weight.reshape(taps, groups * 2 * state_width)
    s_bias = state_bias.reshape(1, groups * 2 * state_width)
    rims = 16
    x_rim, s_rim = shifted(
        (padded_rim(x_input[half - taps + 1 :], rims), padded_rim(s_input[half - taps + 1 :], rims)),
        ("ctx", "sub"),
        1,
    )
    own_raw = lax.dynamic_slice_in_dim(step_raw, sub * heads, heads, 1)
    got_raw = swapped(lax.dynamic_slice_in_dim(step_raw, (1 - sub) * heads, heads, 1), "sub")
    conv = functools.partial(
        conv_half, docs=docs, x=x_input, x_rim=x_rim, w=mix_weight, bias=mix_bias.reshape(1, channels),
        s=s_input, s_rim=s_rim, sw=s_weight, sbias=s_bias, width=width, block=block,
    )
    first = block_first + sub * half
    other = conv(jnp.stack([first, 1 - sub, 1 - sub if whole_groups else zero]))
    got = swapped(other, "sub")
    own = conv(jnp.stack([first, sub, sub if whole_groups else zero]))
    got_gate = swapped(lax.dynamic_slice_in_dim(gate_input, (1 - sub) * width, width, 1), "sub")

    meta = jnp.stack([sub, block_first, tp])
    cols = min(512, group_width)
    steps = width // cols
    rate = lax.dynamic_slice_in_dim(decay_log, sub * heads, heads, 0).reshape(1, heads)
    fixed = lambda *shape: pl.BlockSpec(shape, lambda i, *m: (0,) * len(shape))
    x_cat, bc, state, kept, cum, dlt = pl.pallas_call(
        functools.partial(
            state_kernel, head_width=head_width, group_width=group_width, state_width=state_width
        ),
        grid_spec=pltpu.PrefetchScalarGridSpec(
            num_scalar_prefetch=2,
            grid=(steps,),
            in_specs=[
                pl.BlockSpec((half, cols), lambda i, *m: (0, i)),
                pl.BlockSpec((half, cols), lambda i, *m: (0, i)),
                pl.BlockSpec((half, block), lambda i, *m: (0, width // block)),
                pl.BlockSpec((half, block), lambda i, *m: (0, width // block)),
                fixed(half, heads),
                fixed(half, heads),
                fixed(1, heads),
            ],
            out_specs=[
                pl.BlockSpec((count, cols), lambda i, *m: (0, i)),
                fixed(count, block),
                pl.BlockSpec((state_width, cols), lambda i, *m: (0, i)),
                pl.BlockSpec((8, cols), lambda i, *m: (0, i)),
                fixed(count, heads),
                fixed(heads, count),
            ],
            scratch_shapes=[pltpu.VMEM((count, heads), F32), pltpu.VMEM((2, count, heads), BF16)],
        ),
        out_shape=[
            jax.ShapeDtypeStruct((count, width), BF16),
            jax.ShapeDtypeStruct((count, block), BF16),
            jax.ShapeDtypeStruct((state_width, width), BF16),
            jax.ShapeDtypeStruct((8, width), F32),
            jax.ShapeDtypeStruct((count, heads), F32),
            jax.ShapeDtypeStruct((heads, count), F32),
        ],
        compiler_params=pltpu.CompilerParams(vmem_limit_bytes=32 << 20),
        cost_estimate=pl.CostEstimate(
            flops=4 * count * width * state_width, bytes_accessed=5 * count * width, transcendentals=count * heads
        ),
        name="state",
    )(meta, docs, own, got, own, got, own_raw, got_raw, rate)

    arriving = jnp.zeros_like(state)
    for hop in range(ctx_size // 2):
        leaving = state
        if hop:
            leaving = (state.astype(F32) + kept[:1] * arriving.astype(F32)).astype(BF16)
        arriving = shifted(leaving, "ctx", 1)

    chunks = count // CHUNK
    skip = jnp.repeat(lax.dynamic_slice_in_dim(skip_gain, sub * heads, heads, 0), head_width).reshape(1, width)
    by_row = lambda n: pl.BlockSpec((CHUNK, n), lambda i, *m: (i, 0))
    gated, carry_gate = pl.pallas_call(
        functools.partial(
            intra_kernel, head_width=head_width, group_heads=group_heads, state_width=state_width
        ),
        grid_spec=pltpu.PrefetchScalarGridSpec(
            num_scalar_prefetch=2,
            grid=(chunks,),
            in_specs=[
                by_row(width),
                by_row(block),
                by_row(heads),
                pl.BlockSpec((heads, CHUNK), lambda i, *m: (0, i)),
                pl.BlockSpec((CHUNK, width), lambda i, m, d: (lax.rem(i, chunks // 2), m[0])),
                pl.BlockSpec((CHUNK, width), lambda i, m, d: (lax.rem(i, chunks // 2), 0)),
                fixed(1, width),
            ],
            out_specs=[by_row(width), by_row(width)],
            scratch_shapes=[
                pltpu.VMEM((state_width, width), F32),
                pltpu.VMEM((8, heads), F32),
                pltpu.VMEM((heads, width), BF16),
                pltpu.VMEM((CHUNK, width), F32),
                pltpu.VMEM((CHUNK, width), F32),
                pltpu.VMEM((CHUNK, width), F32),
            ],
        ),
        out_shape=[jax.ShapeDtypeStruct((count, width), F32), jax.ShapeDtypeStruct((count, width), F32)],
        compiler_params=pltpu.CompilerParams(vmem_limit_bytes=32 << 20),
        cost_estimate=pl.CostEstimate(
            flops=8 * count * width * CHUNK, bytes_accessed=14 * count * width,
            transcendentals=count * CHUNK * heads,
        ),
        name="intra",
    )(meta, docs, x_cat, bc, cum, dlt, gate_input, got_gate, skip)

    divisor = HEADS // GROUPS * head_width
    squares = None
    if not whole_groups:
        c = bc[:, state_width:]
        total = gated + jnp.dot(c, arriving, preferred_element_type=F32) * carry_gate
        mine = jnp.sum(total * total, axis=1, keepdims=True)
        squares = mine + swapped(mine, "sub")

    row_steps = chunks
    out_cols = features // tp_size
    mm_cols = min(512, out_cols)
    pair = tp_size == 2
    part = out_cols // mm_cols
    blocks = part if pair else features // mm_cols
    w_first = (lambda m: (1 - m[2]) * part) if pair else (lambda m: 0)
    project = functools.partial(
        project_kernel, row_steps=row_steps, group_width=group_width, state_width=state_width, divisor=divisor
    )
    clamp = lambda i: jnp.minimum(i, row_steps - 1)
    column = lambda i: jnp.maximum(i - row_steps, 0)
    in_specs = [
        pl.BlockSpec((CHUNK, width), lambda i, m: (clamp(i), 0)),
        pl.BlockSpec((CHUNK, width), lambda i, m: (clamp(i), 0)),
        pl.BlockSpec((CHUNK, block), lambda i, m: (clamp(i), 0)),
        fixed(state_width, width),
        pl.BlockSpec((1, width), lambda i, m: (0, m[0])),
    ]
    operands = [gated, carry_gate, bc, arriving, norm_gain.reshape(1, channels)]
    if squares is None:
        body = lambda m, a, f, b, n, g, *rest: project(m, a, f, b, n, g, None, *rest)
    else:
        body = project
        in_specs.append(pl.BlockSpec((CHUNK, 1), lambda i, m: (clamp(i), 0)))
        operands.append(squares)
    in_specs.append(pl.BlockSpec((width, mm_cols), lambda i, m: (0, w_first(m) + column(i))))
    operands.append(out_weight)
    columns = blocks * mm_cols
    hidden, send, keep = pl.pallas_call(
        body,
        grid_spec=pltpu.PrefetchScalarGridSpec(
            num_scalar_prefetch=1,
            grid=(row_steps + blocks,),
            in_specs=in_specs,
            out_specs=[
                fixed(count, width),
                pl.BlockSpec((half, mm_cols), lambda i, m: (0, column(i))),
                pl.BlockSpec((half, mm_cols), lambda i, m: (0, column(i))),
            ],
        ),
        out_shape=[
            jax.ShapeDtypeStruct((count, width), BF16),
            jax.ShapeDtypeStruct((half, columns), BF16),
            jax.ShapeDtypeStruct((half, columns), F32),
        ],
        compiler_params=pltpu.CompilerParams(vmem_limit_bytes=40 << 20),
        cost_estimate=pl.CostEstimate(
            flops=2 * count * width * columns, bytes_accessed=10 * count * width + 2 * width * columns,
            transcendentals=0,
        ),
        name="project",
    )(meta, *operands)
    got_send = swapped(send, "sub")
    far = (keep + got_send.astype(F32)).astype(BF16)
    if not pair:
        return lax.psum_scatter(far, "tp", scatter_dimension=1, tiled=True)
    got_far = swapped(far, "tp")
    near_send, near_keep = pl.pallas_call(
        product_kernel,
        grid_spec=pltpu.PrefetchScalarGridSpec(
            num_scalar_prefetch=1,
            grid=(part,),
            in_specs=[
                fixed(count, width),
                pl.BlockSpec((width, mm_cols), lambda i, m: (0, m[2] * part + i)),
            ],
            out_specs=[
                pl.BlockSpec((half, mm_cols), lambda i, m: (0, i)),
                pl.BlockSpec((half, mm_cols), lambda i, m: (0, i)),
            ],
        ),
        out_shape=[
            jax.ShapeDtypeStruct((half, out_cols), BF16),
            jax.ShapeDtypeStruct((half, out_cols), F32),
        ],
        compiler_params=pltpu.CompilerParams(vmem_limit_bytes=32 << 20),
        cost_estimate=pl.CostEstimate(
            flops=2 * count * width * out_cols, bytes_accessed=2 * count * width + 2 * width * out_cols,
            transcendentals=0,
        ),
        name="product",
    )(meta, hidden, out_weight)
    near = near_keep + swapped(near_send, "sub").astype(F32)
    return (near + got_far.astype(F32)).astype(BF16)


def solution(mesh):
    in_specs = (
        P(("groups", "ctx", "sub"), "tp"),
        P(("groups", "ctx", "sub"), "tp"),
        P(("groups", "ctx", "sub"), "tp", None, None),
        P(None, "tp"),
        P("tp"),
        P(None, "tp", None, None),
        P("tp", None, None),
        P(("groups", "ctx", "sub"), "tp"),
        P("tp"),
        P("tp"),
        P("tp"),
        P(("tp", "sub"), None),
        P("groups"),
    )
    out_specs = P(("groups", "ctx", "sub"), "tp")
    return jax.shard_map(local, mesh=mesh, in_specs=in_specs, out_specs=out_specs, check_vma=False)
```

profile of v0, /device:TPU:0, one launch (start us, length us, event | category | flops | bytes accessed | tf_op | source)
XLA Modules:
  0.0 134.2 jit_solution(17291043838941398389)
XLA Ops:
  0.0 0.9 slice.12
  0.9 2.4 %collective-permute-start = (bf16[16,4096]{1,0:T(8,128)(2,1)S(1)}, bf16[16,4096]{1,0:T(8,128)(2,1)S(1)}, u32[]{:S(2)}, u32[]{:S(2)}) collective-permute-start(bf16[16,4096]{1,0:T(8,128)(2,1)S(1)} %concatenate.6), channel_id=1, source_target_pairs={{0,1},{1,4},{4,5},{5,8},{8,9},{9,12},{12,13},{2,3},{3,6},{6,7},{7,... | collective-permute-start | bytes 393224 | tf_op jit(solution)/shard_map/ppermute | solution.py:23
  4.0 4.6 %collective-permute-start.1 = (bf16[16,1024]{1,0:T(8,128)(2,1)S(1)}, bf16[16,1024]{1,0:T(8,128)(2,1)S(1)}, u32[]{:S(2)}, u32[]{:S(2)}) collective-permute-start(bf16[16,1024]{1,0:T(8,128)(2,1)S(1)} %concatenate.7), channel_id=1, source_target_pairs={{0,1},{1,4},{4,5},{5,8},{8,9},{9,12},{12,13},{2,3},{3,6},{6,7},{7,... | collective-permute-start | bytes 98312 | tf_op jit(solution)/shard_map/ppermute | solution.py:23
  8.7 1.4 %reshape.20.s = bf16[256,1024]{1,0:T(8,128)(2,1)S(1)} reshape(bf16[256,4,2,128]{3,2,1,0:T(2,128)(2,1)} %param.15) | data formatting | bytes 1048576 | tf_op jit(solution)/shard_map/reshape | solution.py:336
  10.8 1.6 %copy-done.2 = bf16[256,4096]{1,0:T(8,128)(2,1)S(1)} copy-done((bf16[256,4096]{1,0:T(8,128)(2,1)S(1)}, bf16[256,4096]{1,0:T(8,128)(2,1)}, u32[]{:S(2)}) %copy-start.2) | copy-done | bytes 2097176
  15.2 4.8 %conv.3 = bf16[256,2560]{1,0:T(8,128)(2,1)} custom-call(s32[3]{0:T(128)S(1)} %pad_add_fusion.2.meta, s32[8]{0:T(128)S(1)} %copy-done.26, bf16[256,4096]{1,0:T(8,128)(2,1)S(1)} %copy-done.2, bf16[16,4096]{1,0:T(8,128)(2,1)S(1)} %collective-permute-done.x_rim, bf16[4,4096]{1,0:T(4,128)(2,1)S(1)} %copy-done.15, f32[1,4096]{1,0:T(1,128)S(1)} %bitcast.11, ...), custom_call_target="tpu_custom_call" | custom-call | flops 4194304 | bytes 2621440 | tf_op jit(solution)/shard_map/conv/pallas_call | solution.py:130
  20.0 0.8 copy-done.5
  21.4 1.4 %constant_dynamic-slice_fusion.1 = (f32[256,32]{0,1:T(8,128)}, f32[256,32]{0,1:T(8,128)}) fusion(f32[256,64]{0,1:T(8,128)} %param.20, s32[]{:T(128)S(6)} %select_n.12, s32[]{:T(128)S(6)} %select_n.11), kind=kLoop, calls=%fused_computation.4 | loop fusion | bytes 131080 | tf_op jit(solution)/shard_map/dynamic_slice | solution.py:346
  22.8 1.5 %copy.17 = f32[256,32]{1,0:T(8,128)} copy(f32[256,32]{0,1:T(8,128)} %get-tuple-element.31) | data formatting | bytes 65536
  26.7 1.5 %copy.16.own_raw = f32[256,32]{1,0:T(8,128)} copy(f32[256,32]{0,1:T(8,128)} %get-tuple-element.32) | data formatting | bytes 65536
  28.2 1.0 copy-done.6
  29.2 0.8 copy-done.16
  30.0 0.8 copy-done.18
  32.8 4.0 %conv.2.own.own_bc = bf16[256,2560]{1,0:T(8,128)(2,1)S(1)} custom-call(s32[3]{0:T(128)S(1)} %copy-done.31, s32[8]{0:T(128)S(1)} %copy-done.27, bf16[256,4096]{1,0:T(8,128)(2,1)S(1)} %copy-done.3, bf16[16,4096]{1,0:T(8,128)(2,1)S(1)} %collective-permute-done.x_rim, bf16[4,4096]{1,0:T(4,128)(2,1)S(1)} %copy-done.16, f32[1,4096]{1,0:T(1,128)S(1)} %bitcast.12, ...), custom_call_target="tpu_custom_call" | custom-call | flops 4194304 | bytes 2621440 | tf_op jit(solution)/shard_map/conv/pallas_call | solution.py:130
  36.8 5.8 %state.1 = (bf16[512,2048]{1,0:T(8,128)(2,1)S(1)}, bf16[512,512]{1,0:T(8,128)(2,1)S(1)}, bf16[128,2048]{1,0:T(8,128)(2,1)}, f32[8,2048]{1,0:T(8,128)S(1)}, f32[512,32]{1,0:T(8,128)S(1)}, /*index=5*/f32[32,512]{1,0:T(8,128)S(1)}) custom-call(s32[3]{0:T(128)S(1)} %copy-done.24, s32[8]{0:T(128)S(1)} %copy-done.27, bf16[256,2560]{1,0:T(8,128)(2,1)S(1)} %conv.2.own.own_bc, ...), custom_call_target="tpu_custom_call" | custom-call | flops 536870912 | bytes 5242880 | tf_op jit(solution)/shard_map/state/pallas_call | solution.py:362
  42.7 0.8 copy-done.8
  43.4 1.3 copy-done.10
  46.1 3.6 %collective-permute-start.5 = (bf16[128,2048]{1,0:T(8,128)(2,1)}, bf16[128,2048]{1,0:T(8,128)(2,1)S(1)}, u32[]{:S(2)}, u32[]{:S(2)}) collective-permute-start(bf16[128,2048]{1,0:T(8,128)(2,1)} %get-tuple-element.24), channel_id=1, source_target_pairs={{0,4},{4,8},{8,12},{1,5},{5,9},{9,13},{2,6},{6,10},{10,14},{3,7},{... | collective-permute-start | bytes 1572872 | tf_op jit(solution)/shard_map/ppermute | solution.py:23
  49.8 1.0 constant_dynamic-slice_fusion
  50.9 0.8 slice.15
  51.7 9.7 %collective-permute-done.5 = bf16[128,2048]{1,0:T(8,128)(2,1)S(1)} collective-permute-done((bf16[128,2048]{1,0:T(8,128)(2,1)}, bf16[128,2048]{1,0:T(8,128)(2,1)S(1)}, u32[]{:S(2)}, u32[]{:S(2)}) %collective-permute-start.5) | collective-permute-done | bytes 524320 | tf_op jit(solution)/shard_map/ppermute | solution.py:23
  61.4 2.0 %add_convert_fusion.2 = bf16[128,2048]{1,0:T(8,128)(2,1)} fusion(bf16[128,2048]{1,0:T(8,128)(2,1)S(1)} %collective-permute-done.5, bf16[128,2048]{1,0:T(8,128)(2,1)} %get-tuple-element.24, f32[2048]{0:T(1024)S(1)} %bitcast.16), kind=kLoop, calls=%fused_computation.2 | loop fusion | flops 1310720 | bytes 1581056 | tf_op jit(solution)/shard_map/convert_element_type | solution.py:407
  63.4 4.3 %collective-permute-start.6 = (bf16[128,2048]{1,0:T(8,128)(2,1)}, bf16[128,2048]{1,0:T(8,128)(2,1)S(1)}, u32[]{:S(2)}, u32[]{:S(2)}) collective-permute-start(bf16[128,2048]{1,0:T(8,128)(2,1)} %add_convert_fusion.2), channel_id=1, source_target_pairs={{0,4},{4,8},{8,12},{1,5},{5,9},{9,13},{2,6},{6,10},{10,14},{3,7},{... | collective-permute-start | bytes 1572872 | tf_op jit(solution)/shard_map/ppermute | solution.py:23
  68.0 1.6 %copy-done.11 = bf16[512,2048]{1,0:T(8,128)(2,1)S(1)} copy-done((bf16[512,2048]{1,0:T(8,128)(2,1)S(1)}, bf16[512,2048]{1,0:T(8,128)(2,1)}, u32[]{:S(2)}) %copy-start.11) | copy-done | bytes 2097176
  69.6 11.4 %intra.1 = (f32[512,2048]{1,0:T(8,128)S(1)}, f32[512,2048]{1,0:T(8,128)S(1)}) custom-call(s32[3]{0:T(128)S(1)} %copy-done.25, s32[8]{0:T(128)S(1)} %copy-done.28, bf16[512,2048]{1,0:T(8,128)(2,1)S(1)} %copy-done.11, bf16[512,512]{1,0:T(8,128)(2,1)S(1)} %copy-done.9, f32[512,32]{1,0:T(8,128)S(1)} %copy-done.14, f32[32,512]{1,0:T(8,128)S(1)} %get-tuple-element.21.dlt, ...), custom_call_target="tpu_custom_call" | custom-call | flops 1073741824 | bytes 14680064 | tf_op jit(solution)/shard_map/intra/pallas_call | solution.py:413
  81.1 2.0 %copy-done.7 = f32[512,2048]{1,0:T(8,128)} copy-done((f32[512,2048]{1,0:T(8,128)}, f32[512,2048]{1,0:T(8,128)S(1)}, u32[]{:S(2)}) %copy-start.7) | copy-done | bytes 4194328
  83.0 11.2 %project.1 = (bf16[512,2048]{1,0:T(8,128)(2,1)S(1)}, bf16[256,2048]{1,0:T(8,128)(2,1)S(1)}, f32[256,2048]{1,0:T(8,128)S(1)}) custom-call(s32[3]{0:T(128)S(1)} %copy-done.25, f32[512,2048]{1,0:T(8,128)S(1)} %get-tuple-element.22.a, f32[512,2048]{1,0:T(8,128)} %copy-done.7, bf16[512,512]{1,0:T(8,128)(2,1)S(1)} %copy-done.9, ...), custom_call_target="tpu_custom_call" | custom-call | flops 4294967296 | bytes 18874368 | tf_op jit(solution)/shard_map/project/pallas_call | solution.py:485
  94.3 5.8 %copy-done.1 = bf16[2048,4096]{1,0:T(8,128)(2,1)S(1)} copy-done((bf16[2048,4096]{1,0:T(8,128)(2,1)S(1)}, bf16[2048,4096]{1,0:T(8,128)(2,1)}, u32[]{:S(2)}) %copy-start.1) | copy-done | bytes 16777240
  100.1 6.6 %product.1 = (bf16[256,2048]{1,0:T(8,128)(2,1)S(1)}, f32[256,2048]{1,0:T(8,128)S(1)}) custom-call(s32[3]{0:T(128)S(1)} %copy-done.25, bf16[512,2048]{1,0:T(8,128)(2,1)S(1)} %get-tuple-element.26.hidden, bf16[2048,4096]{1,0:T(8,128)(2,1)S(1)} %copy-done.1), custom_call_target="tpu_custom_call" | custom-call | flops 4294967296 | bytes 10485760 | tf_op jit(solution)/shard_map/product/pallas_call | solution.py:514
  107.6 1.6 %collective-permute-start.9 = (bf16[256,2048]{1,0:T(8,128)(2,1)S(1)}, bf16[256,2048]{1,0:T(8,128)(2,1)S(1)}, u32[]{:S(2)}, u32[]{:S(2)}) collective-permute-start(bf16[256,2048]{1,0:T(8,128)(2,1)S(1)} %add_convert_fusion.1), channel_id=1, source_target_pairs={{0,2},{2,0},{1,3},{3,1},{4,6},{6,4},{5,7},{7,5},{8,10},{10,8},{9,1... | collective-permute-start | bytes 3145736 | tf_op jit(solution)/shard_map/ppermute | solution.py:27
  109.5 23.2 %collective-permute-done.9 = bf16[256,2048]{1,0:T(8,128)(2,1)S(1)} collective-permute-done((bf16[256,2048]{1,0:T(8,128)(2,1)S(1)}, bf16[256,2048]{1,0:T(8,128)(2,1)S(1)}, u32[]{:S(2)}, u32[]{:S(2)}) %collective-permute-start.9) | collective-permute-done | bytes 1048608 | tf_op jit(solution)/shard_map/ppermute | solution.py:27
  132.7 1.4 %add_convert_fusion = bf16[256,2048]{1,0:T(8,128)(2,1)} fusion(bf16[256,2048]{1,0:T(8,128)(2,1)S(1)} %collective-permute-done.9, f32[256,2048]{1,0:T(8,128)S(1)} %get-tuple-element.27, bf16[256,2048]{1,0:T(8,128)(2,1)S(1)} %collective-permute-done.7), kind=kLoop, calls=%fused_computation | loop fusion | flops 2621440 | bytes 5242880 | tf_op jit(solution)/shard_map/convert_element_type | solution.py:540
  (82 shorter events, 12.3 us)
Async XLA Ops:
  0.0 25.4 %copy-start = (f32[64]{0:T(128)S(1)}, f32[64]{0:T(128)}, u32[]{:S(2)}) copy-start(f32[64]{0:T(128)} %param.21) | copy-start | bytes 772
  0.9 9.9 %collective-permute-start = (bf16[16,4096]{1,0:T(8,128)(2,1)S(1)}, bf16[16,4096]{1,0:T(8,128)(2,1)S(1)}, u32[]{:S(2)}, u32[]{:S(2)}) collective-permute-start(bf16[16,4096]{1,0:T(8,128)(2,1)S(1)} %concatenate.6), channel_id=1, source_target_pairs={{0,1},{1,4},{4,5},{5,8},{8,9},{9,12},{12,13},{2,3},{3,6},{6,7},{7,... | collective-permute-start | bytes 393224 | tf_op jit(solution)/shard_map/ppermute | solution.py:23
  4.0 6.8 %collective-permute-start.1 = (bf16[16,1024]{1,0:T(8,128)(2,1)S(1)}, bf16[16,1024]{1,0:T(8,128)(2,1)S(1)}, u32[]{:S(2)}, u32[]{:S(2)}) collective-permute-start(bf16[16,1024]{1,0:T(8,128)(2,1)S(1)} %concatenate.7), channel_id=1, source_target_pairs={{0,1},{1,4},{4,5},{5,8},{8,9},{9,12},{12,13},{2,3},{3,6},{6,7},{7,... | collective-permute-start | bytes 98312 | tf_op jit(solution)/shard_map/ppermute | solution.py:23
  10.8 1.6 %copy-start.2 = (bf16[256,4096]{1,0:T(8,128)(2,1)S(1)}, bf16[256,4096]{1,0:T(8,128)(2,1)}, u32[]{:S(2)}) copy-start(bf16[256,4096]{1,0:T(8,128)(2,1)} %x.7) | copy-start | bytes 6291460
  12.4 0.8 copy-start.15
  15.2 12.9 %copy-start.3 = (bf16[256,4096]{1,0:T(8,128)(2,1)S(1)}, bf16[256,4096]{1,0:T(8,128)(2,1)}, u32[]{:S(2)}) copy-start(bf16[256,4096]{1,0:T(8,128)(2,1)} %x.7) | copy-start | bytes 6291460
  15.2 12.9 %copy-start.23 = (f32[4,2,128]{2,1,0:T(2,128)S(1)}, f32[4,2,128]{2,1,0:T(2,128)}, u32[]{:S(2)}) copy-start(f32[4,2,128]{2,1,0:T(2,128)} %param.19) | copy-start | bytes 12292
  20.0 0.8 copy-start.5
  21.4 15.4 %collective-permute-start.2 = (bf16[256,2560]{1,0:T(8,128)(2,1)}, bf16[256,2560]{1,0:T(8,128)(2,1)S(1)}, u32[]{:S(2)}, u32[]{:S(2)}) collective-permute-start(bf16[256,2560]{1,0:T(8,128)(2,1)} %conv.3), channel_id=1, source_target_pairs={{0,1},{1,0},{2,3},{3,2},{4,5},{5,4},{6,7},{7,6},{8,9},{9,8},{10,11... | collective-permute-start | bytes 3932168 | tf_op jit(solution)/shard_map/ppermute | solution.py:27
  24.3 12.5 %collective-permute-start.3 = (f32[256,32]{1,0:T(8,128)}, f32[256,32]{1,0:T(8,128)}, u32[]{:S(2)}, u32[]{:S(2)}) collective-permute-start(f32[256,32]{1,0:T(8,128)} %copy.17), channel_id=1, source_target_pairs={{0,1},{1,0},{2,3},{3,2},{4,5},{5,4},{6,7},{7,6},{8,9},{9,8},{10,11... | collective-permute-start | bytes 98312 | tf_op jit(solution)/shard_map/ppermute | solution.py:27
  28.2 1.0 copy-start.6
  32.7 4.0 %copy-start.12 = (f32[256,32]{1,0:T(8,128)S(1)}, f32[256,32]{1,0:T(8,128)}, u32[]{:S(2)}) copy-start(f32[256,32]{1,0:T(8,128)} %copy.16.own_raw) | copy-start | bytes 98308
  32.7 4.0 %copy-start.24 = (s32[3]{0:T(128)S(1)}, s32[3]{0:T(128)}, u32[]{:S(2)}) copy-start(s32[3]{0:T(128)} %pad_add_fusion.meta.m) | copy-start | bytes 40
  32.8 4.1 %copy-start.30 = (f32[1,32]{1,0:T(1,128)S(1)}, f32[1,32]{1,0:T(1,128)}, u32[]{:S(2)}) copy-start(f32[1,32]{1,0:T(1,128)} %dynamic-slice_bitcast_fusion.rate) | copy-start | bytes 388
  36.8 13.1 %copy-start.4 = (bf16[256,4096]{1,0:T(8,128)(2,1)S(1)}, bf16[256,4096]{1,0:T(8,128)(2,1)}, u32[]{:S(2)}) copy-start(bf16[256,4096]{1,0:T(8,128)(2,1)} %gate_own.1) | copy-start | bytes 6291460
  42.6 0.8 copy-start.8
  43.4 1.3 %copy-start.10 = (bf16[512,2048]{1,0:T(8,128)(2,1)}, bf16[512,2048]{1,0:T(8,128)(2,1)S(1)}, u32[]{:S(2)}) copy-start(bf16[512,2048]{1,0:T(8,128)(2,1)S(1)} %get-tuple-element.18.x) | copy-start | bytes 6291460
  46.1 21.6 %copy-start.32 = (f32[64]{0:T(128)S(1)}, f32[64]{0:T(128)}, u32[]{:S(2)}) copy-start(f32[64]{0:T(128)} %param.22) | copy-start | bytes 772
  46.1 21.9 %copy-start.25 = (s32[3]{0:T(128)S(1)}, s32[3]{0:T(128)}, u32[]{:S(2)}) copy-start(s32[3]{0:T(128)} %pad_add_fusion.meta.m) | copy-start | bytes 40
  46.1 21.9 %copy-start.28 = (s32[8]{0:T(128)S(1)}, s32[8]{0:T(128)}, u32[]{:S(2)}) copy-start(s32[8]{0:T(128)} %docs.7) | copy-start | bytes 100
  46.1 21.9 %copy-start.9 = (bf16[512,512]{1,0:T(8,128)(2,1)S(1)}, bf16[512,512]{1,0:T(8,128)(2,1)}, u32[]{:S(2)}) copy-start(bf16[512,512]{1,0:T(8,128)(2,1)} %copy-done.8) | copy-start | bytes 1572868
  46.1 21.9 %copy-start.14 = (f32[512,32]{1,0:T(8,128)S(1)}, f32[512,32]{1,0:T(8,128)}, u32[]{:S(2)}) copy-start(f32[512,32]{1,0:T(8,128)} %copy-done.13) | copy-start | bytes 196612
  46.1 15.3 %collective-permute-start.5 = (bf16[128,2048]{1,0:T(8,128)(2,1)}, bf16[128,2048]{1,0:T(8,128)(2,1)S(1)}, u32[]{:S(2)}, u32[]{:S(2)}) collective-permute-start(bf16[128,2048]{1,0:T(8,128)(2,1)} %get-tuple-element.24), channel_id=1, source_target_pairs={{0,4},{4,8},{8,12},{1,5},{5,9},{9,13},{2,6},{6,10},{10,14},{3,7},{... | collective-permute-start | bytes 1572872 | tf_op jit(solution)/shard_map/ppermute | solution.py:23
  50.9 17.1 %collective-permute-start.4 = (bf16[256,2048]{1,0:T(8,128)(2,1)}, bf16[256,2048]{1,0:T(8,128)(2,1)}, u32[]{:S(2)}, u32[]{:S(2)}) collective-permute-start(bf16[256,2048]{1,0:T(8,128)(2,1)} %constant_dynamic-slice_fusion), channel_id=1, source_target_pairs={{0,1},{1,0},{2,3},{3,2},{4,5},{5,4},{6,7},{7,6},{8,9},{9,8},{10,11... | collective-permute-start | bytes 3145736 | tf_op jit(solution)/shard_map/ppermute | solution.py:27
  63.4 19.6 %collective-permute-start.6 = (bf16[128,2048]{1,0:T(8,128)(2,1)}, bf16[128,2048]{1,0:T(8,128)(2,1)S(1)}, u32[]{:S(2)}, u32[]{:S(2)}) collective-permute-start(bf16[128,2048]{1,0:T(8,128)(2,1)} %add_convert_fusion.2), channel_id=1, source_target_pairs={{0,4},{4,8},{8,12},{1,5},{5,9},{9,13},{2,6},{6,10},{10,14},{3,7},{... | collective-permute-start | bytes 1572872 | tf_op jit(solution)/shard_map/ppermute | solution.py:23
  68.0 1.6 %copy-start.11 = (bf16[512,2048]{1,0:T(8,128)(2,1)S(1)}, bf16[512,2048]{1,0:T(8,128)(2,1)}, u32[]{:S(2)}) copy-start(bf16[512,2048]{1,0:T(8,128)(2,1)} %copy-done.10) | copy-start | bytes 6291460
  69.6 13.4 %copy-start.21 = (f32[4096]{0:T(1024)S(1)}, f32[4096]{0:T(1024)}, u32[]{:S(2)}) copy-start(f32[4096]{0:T(1024)} %param.23) | copy-start | bytes 49156
  81.0 2.0 %copy-start.7 = (f32[512,2048]{1,0:T(8,128)}, f32[512,2048]{1,0:T(8,128)S(1)}, u32[]{:S(2)}) copy-start(f32[512,2048]{1,0:T(8,128)S(1)} %get-tuple-element.23.f) | copy-start | bytes 12582916
  94.2 13.0 %collective-permute-start.8 = (bf16[256,2048]{1,0:T(8,128)(2,1)S(1)}, bf16[256,2048]{1,0:T(8,128)(2,1)S(1)}, u32[]{:S(2)}, u32[]{:S(2)}) collective-permute-start(bf16[256,2048]{1,0:T(8,128)(2,1)S(1)} %get-tuple-element.30), channel_id=1, source_target_pairs={{0,1},{1,0},{2,3},{3,2},{4,5},{5,4},{6,7},{7,6},{8,9},{9,8},{10,11... | collective-permute-start | bytes 3145736 | tf_op jit(solution)/shard_map/ppermute | solution.py:27
  94.3 5.8 %copy-start.1 = (bf16[2048,4096]{1,0:T(8,128)(2,1)S(1)}, bf16[2048,4096]{1,0:T(8,128)(2,1)}, u32[]{:S(2)}) copy-start(bf16[2048,4096]{1,0:T(8,128)(2,1)} %w.5) | copy-start | bytes 50331652
  106.7 2.8 %collective-permute-start.7 = (bf16[256,2048]{1,0:T(8,128)(2,1)S(1)}, bf16[256,2048]{1,0:T(8,128)(2,1)S(1)}, u32[]{:S(2)}, u32[]{:S(2)}) collective-permute-start(bf16[256,2048]{1,0:T(8,128)(2,1)S(1)} %get-tuple-element.28), channel_id=1, source_target_pairs={{0,1},{1,0},{2,3},{3,2},{4,5},{5,4},{6,7},{7,6},{8,9},{9,8},{10,11... | collective-permute-start | bytes 3145736 | tf_op jit(solution)/shard_map/ppermute | solution.py:27
  107.6 25.2 %collective-permute-start.9 = (bf16[256,2048]{1,0:T(8,128)(2,1)S(1)}, bf16[256,2048]{1,0:T(8,128)(2,1)S(1)}, u32[]{:S(2)}, u32[]{:S(2)}) collective-permute-start(bf16[256,2048]{1,0:T(8,128)(2,1)S(1)} %add_convert_fusion.1), channel_id=1, source_target_pairs={{0,2},{2,0},{1,3},{3,1},{4,6},{6,4},{5,7},{7,5},{8,10},{10,8},{9,1... | collective-permute-start | bytes 3145736 | tf_op jit(solution)/shard_map/ppermute | solution.py:27
  (11 other events, 7.5 us)
where the time goes:
time: 135 us; the launch traced here: 134 us
  Pallas kernels  43.8 us (32%)
  local copies, waits for them, and re-layouts  34 us (25%)
  waiting for transfers between devices  33.3 us (25%)
  starting transfers between devices  17.6 us (13%)
  other arithmetic  5.12 us (4%)
    unnamed x68, local copies, waits for them, and re-layouts  26.2 us
    ppermute x6, waiting for transfers between devices, swapped(): lax.ppermute(shard, axis, [(i, i ^ 1) for i in range(lax.axis_size(axis))])  23.6 us
    ppermute x4, starting transfers between devices, shifted(): return lax.ppermute(shard, axis, pairs)  14.9 us
    pallas_call x1, Pallas kernels, local(): pl.pallas_call(functools.partial(intra_kernel, head_width=head_width, gro...  11.4 us
    pallas_call x1, Pallas kernels, local(): pl.pallas_call(body, grid_spec=pltpu.PrefetchScalarGridSpec(num_scalar_pr...  11.2 us
    ppermute x4, waiting for transfers between devices, shifted(): return lax.ppermute(shard, axis, pairs)  9.73 us
    pallas_call x2, Pallas kernels, conv_half(): pl.pallas_call(functools.partial(conv_kernel, taps=taps), grid_spec=pltpu...  8.75 us
    pallas_call x1, Pallas kernels, local(): pl.pallas_call(product_kernel, grid_spec=pltpu.PrefetchScalarGridSpec(num...  6.61 us
  transfers between devices with their start and end apart: 10, of which 3 were waited for; matrix products, arithmetic and copies ran while one was open for 10% of the time, Pallas kernels for 16%

commit v1 on v0

--- a/solution.py
+++ b/solution.py
@@ -13,6 +13,7 @@
 EPSILON = 1e-05
 LOG2E = 1.4426950408889634
 MASKED = -1e30
+VMEM = 60 << 20
 F32 = jnp.float32
 BF16 = jnp.bfloat16
 
@@ -83,7 +84,8 @@
 
     @pl.when(step == 0)
     def _():
-        start = doc_start(rows_of(count, meta[0]), docs) - meta[0]
+        first = meta[1] + meta[0] * count
+        start = doc_start(rows_of(count, first), docs) - first
         row = lax.broadcasted_iota(jnp.int32, (count, count), 0)
         col = lax.broadcasted_iota(jnp.int32, (count, count), 1)
         rim_row = lax.broadcasted_iota(jnp.int32, (rims, rims), 0)
@@ -116,17 +118,19 @@
         mix(s, s_rim, sw, sbias)
 
 
-def conv_half(meta, docs, x, x_rim, w, bias, s, s_rim, sw, sbias, width, block):
-    count = x.shape[0]
+def conv_half(other, meta, docs, x, w, bias, s, sw, sbias, rim, rims, width, block, whole_groups):
+    count, channels = x.shape
     taps = w.shape[0]
-    rims = x_rim.shape[0]
     steps = width // block
-    x_at = lambda i, m, d: (0, m[1] * steps + jnp.minimum(i, steps - 1))
-    s_at = lambda i, m, d: (0, m[2])
+    half = lambda m: 1 - m[0] if other else m[0]
+    x_at = lambda i, m, d: half(m) * steps + jnp.minimum(i, steps - 1)
+    s_at = lambda i, m, d: half(m) if whole_groups else 0
+    rim_at = lambda i, m, d: channels // block + s_at(i, m, d)
     specs = []
-    for at in (x_at, s_at):
+    for at, rim_col in ((x_at, x_at), (s_at, rim_at)):
         for rows in (count, rims, taps, 1):
-            specs.append(pl.BlockSpec((rows, block), at))
+            col = rim_col if rows == rims else at
+            specs.append(pl.BlockSpec((rows, block), lambda i, m, d, col=col: (0, col(i, m, d))))
     return pl.pallas_call(
         functools.partial(conv_kernel, taps=taps),
         grid_spec=pltpu.PrefetchScalarGridSpec(
@@ -140,12 +144,12 @@
             ],
         ),
         out_shape=jax.ShapeDtypeStruct((count, width + block), BF16),
-        compiler_params=pltpu.CompilerParams(vmem_limit_bytes=32 << 20),
+        compiler_params=pltpu.CompilerParams(vmem_limit_bytes=VMEM),
         cost_estimate=pl.CostEstimate(
             flops=8 * count * width, bytes_accessed=4 * count * (width + block), transcendentals=count * width
         ),
         name="conv",
-    )(meta, docs, x, x_rim, w, bias, s, s_rim, sw, sbias)
+    )(meta, docs, x, rim, w, bias, s, rim, sw, sbias)
 
 
 def state_kernel(
@@ -167,11 +171,13 @@
     def _():
         bc_out[own_at, :] = own_bc[...]
         bc_out[got_at, :] = got_bc[...]
-        raw[own_at, :] = own_raw[...]
-        raw[got_at, :] = got_raw[...]
+        mine = meta[0] == 0
+        raw[own_at, :] = jnp.where(mine, own_raw[:, :heads], own_raw[:, heads:])
+        raw[got_at, :] = jnp.where(mine, got_raw[:, :heads], got_raw[:, heads:])
         value = raw[...]
+        rates = jnp.where(mine, rate[:, :heads], rate[:, heads:])
         size = jnp.maximum(value, 0.0) + jnp.log(1.0 + jnp.exp(-jnp.abs(value)))
-        decay = (-LOG2E * jnp.exp(rate[...])) * size
+        decay = (-LOG2E * jnp.exp(rates)) * size
         row = lax.broadcasted_iota(jnp.int32, (count, count), 0)
         col = lax.broadcasted_iota(jnp.int32, (count, count), 1)
         below = jnp.where(col <= row, 1.0, 0.0).astype(BF16)
@@ -199,8 +205,8 @@
 
 
 def intra_kernel(
-    meta, docs, x, bc, cum, dlt, gate_own, gate_got, skip,
-    a_out, f_out, state, base, spread, reach, into, tail,
+    meta, docs, x, bc, cum, dlt, gate_own, gate_got, gain,
+    a_out, f_out, state, base, spread, skip, reach, into, tail,
     *, head_width, group_heads, state_width,
 ):
     step = pl.program_id(0)
@@ -213,6 +219,9 @@
         state[...] = jnp.zeros_like(state)
         base[...] = jnp.zeros_like(base)
         spread[...] = head_lanes(heads, head_width, width, 0)
+        mine = jnp.where(meta[0] == 0, gain[:, :heads], gain[:, heads:])
+        high, mid, low = split3(jnp.broadcast_to(mine, (8, heads)))
+        skip[...] = mm(high, spread[...]) + (mm(mid, spread[...]) + mm(low, spread[...]))
 
     starts = doc_start(rows_of(count, first), docs)
     last_start = doc_start(first + count - 1, docs)
@@ -254,7 +263,7 @@
             old = state[:, at]
             carried = mm(c, old.astype(BF16)) * reach[:, at]
             x_part = value.astype(F32)
-            y = within + carried + x_part * skip[:, at]
+            y = within + carried + x_part * skip[:1, at]
             gate = silu(jnp.where(is_own, gate_own[:, at], gate_got[:, at]).astype(F32))
             a_out[:, at] = y * gate
             f_out[:, at] = gate * into[:, at]
@@ -300,10 +309,6 @@
     here = pl.ds(pl.multiple_of(meta[0] * half, half), half)
     send[...] = mm(hidden[there, :], w[...]).astype(BF16)
     keep[...] = mm(hidden[here, :], w[...])
-
-
-def padded_rim(shard, rims):
-    return jnp.concatenate([jnp.zeros((rims - shard.shape[0],) + shard.shape[1:], shard.dtype), shard])
 
 
 def local(
@@ -331,33 +336,25 @@
     ctx_size = lax.axis_size("ctx")
     block_first = ctx * count
     docs = doc_lengths.astype(jnp.int32)
-    zero = jnp.int32(0)
 
     s_input = state_proj.reshape(half, groups * 2 * state_width)
     s_weight = state_weight.reshape(taps, groups * 2 * state_width)
     s_bias = state_bias.reshape(1, groups * 2 * state_width)
     rims = 16
-    x_rim, s_rim = shifted(
-        (padded_rim(x_input[half - taps + 1 :], rims), padded_rim(s_input[half - taps + 1 :], rims)),
-        ("ctx", "sub"),
-        1,
+    meta = jnp.stack([sub, block_first, tp])
+    rim = shifted(jnp.concatenate([x_input[half - rims :], s_input[half - rims :]], axis=1), ("ctx", "sub"), 1)
+    got_raw = swapped(step_raw, "sub")
+    conv = functools.partial(
+        conv_half, meta=meta, docs=docs, x=x_input, w=mix_weight, bias=mix_bias.reshape(1, channels), s=s_input,
+        sw=s_weight, sbias=s_bias, rim=rim, rims=rims, width=width, block=block, whole_groups=whole_groups,
     )
-    own_raw = lax.dynamic_slice_in_dim(step_raw, sub * heads, heads, 1)
-    got_raw = swapped(lax.dynamic_slice_in_dim(step_raw, (1 - sub) * heads, heads, 1), "sub")
-    conv = functools.partial(
-        conv_half, docs=docs, x=x_input, x_rim=x_rim, w=mix_weight, bias=mix_bias.reshape(1, channels),
-        s=s_input, s_rim=s_rim, sw=s_weight, sbias=s_bias, width=width, block=block,
-    )
-    first = block_first + sub * half
-    other = conv(jnp.stack([first, 1 - sub, 1 - sub if whole_groups else zero]))
+    other = conv(True)
     got = swapped(other, "sub")
-    own = conv(jnp.stack([first, sub, sub if whole_groups else zero]))
+    own = conv(False)
     got_gate = swapped(lax.dynamic_slice_in_dim(gate_input, (1 - sub) * width, width, 1), "sub")
 
-    meta = jnp.stack([sub, block_first, tp])
     cols = min(512, group_width)
     steps = width // cols
-    rate = lax.dynamic_slice_in_dim(decay_log, sub * heads, heads, 0).reshape(1, heads)
     fixed = lambda *shape: pl.BlockSpec(shape, lambda i, *m: (0,) * len(shape))
     x_cat, bc, state, kept, cum, dlt = pl.pallas_call(
         functools.partial(
@@ -371,9 +368,9 @@
                 pl.BlockSpec((half, cols), lambda i, *m: (0, i)),
                 pl.BlockSpec((half, block), lambda i, *m: (0, width // block)),
                 pl.BlockSpec((half, block), lambda i, *m: (0, width // block)),
-                fixed(half, heads),
-                fixed(half, heads),
-                fixed(1, heads),
+                fixed(half, all_heads),
+                fixed(half, all_heads),
+                fixed(1, all_heads),
             ],
             out_specs=[
                 pl.BlockSpec((count, cols), lambda i, *m: (0, i)),
@@ -393,12 +390,12 @@
             jax.ShapeDtypeStruct((count, heads), F32),
             jax.ShapeDtypeStruct((heads, count), F32),
         ],
-        compiler_params=pltpu.CompilerParams(vmem_limit_bytes=32 << 20),
+        compiler_params=pltpu.CompilerParams(vmem_limit_bytes=VMEM),
         cost_estimate=pl.CostEstimate(
             flops=4 * count * width * state_width, bytes_accessed=5 * count * width, transcendentals=count * heads
         ),
         name="state",
-    )(meta, docs, own, got, own, got, own_raw, got_raw, rate)
+    )(meta, docs, own, got, own, got, step_raw, got_raw, decay_log.reshape(1, all_heads))
 
     arriving = jnp.zeros_like(state)
     for hop in range(ctx_size // 2):
@@ -408,7 +405,6 @@
         arriving = shifted(leaving, "ctx", 1)
 
     chunks = count // CHUNK
-    skip = jnp.repeat(lax.dynamic_slice_in_dim(skip_gain, sub * heads, heads, 0), head_width).reshape(1, width)
     by_row = lambda n: pl.BlockSpec((CHUNK, n), lambda i, *m: (i, 0))
     gated, carry_gate = pl.pallas_call(
         functools.partial(
@@ -424,26 +420,27 @@
                 pl.BlockSpec((heads, CHUNK), lambda i, *m: (0, i)),
                 pl.BlockSpec((CHUNK, width), lambda i, m, d: (lax.rem(i, chunks // 2), m[0])),
                 pl.BlockSpec((CHUNK, width), lambda i, m, d: (lax.rem(i, chunks // 2), 0)),
-                fixed(1, width),
+                fixed(1, all_heads),
             ],
             out_specs=[by_row(width), by_row(width)],
             scratch_shapes=[
                 pltpu.VMEM((state_width, width), F32),
                 pltpu.VMEM((8, heads), F32),
                 pltpu.VMEM((heads, width), BF16),
+                pltpu.VMEM((8, width), F32),
                 pltpu.VMEM((CHUNK, width), F32),
                 pltpu.VMEM((CHUNK, width), F32),
                 pltpu.VMEM((CHUNK, width), F32),
             ],
         ),
         out_shape=[jax.ShapeDtypeStruct((count, width), F32), jax.ShapeDtypeStruct((count, width), F32)],
-        compiler_params=pltpu.CompilerParams(vmem_limit_bytes=32 << 20),
+        compiler_params=pltpu.CompilerParams(vmem_limit_bytes=VMEM),
         cost_estimate=pl.CostEstimate(
             flops=8 * count * width * CHUNK, bytes_accessed=14 * count * width,
             transcendentals=count * CHUNK * heads,
         ),
         name="intra",
-    )(meta, docs, x_cat, bc, cum, dlt, gate_input, got_gate, skip)
+    )(meta, docs, x_cat, bc, cum, dlt, gate_input, got_gate, skip_gain.reshape(1, all_heads))
 
     divisor = HEADS // GROUPS * head_width
     squares = None
@@ -499,7 +496,7 @@
             jax.ShapeDtypeStruct((half, columns), BF16),
             jax.ShapeDtypeStruct((half, columns), F32),
         ],
-        compiler_params=pltpu.CompilerParams(vmem_limit_bytes=40 << 20),
+        compiler_params=pltpu.CompilerParams(vmem_limit_bytes=VMEM),
         cost_estimate=pl.CostEstimate(
             flops=2 * count * width * columns, bytes_accessed=10 * count * width + 2 * width * columns,
             transcendentals=0,
@@ -529,7 +526,7 @@
             jax.ShapeDtypeStruct((half, out_cols), BF16),
             jax.ShapeDtypeStruct((half, out_cols), F32),
         ],
-        compiler_params=pltpu.CompilerParams(vmem_limit_bytes=32 << 20),
+        compiler_params=pltpu.CompilerParams(vmem_limit_bytes=VMEM),
         cost_estimate=pl.CostEstimate(
             flops=2 * count * width * out_cols, bytes_accessed=2 * count * width + 2 * width * out_cols,
             transcendentals=0,

time: 135 us -> 119 us (0.88)
  local copies, waits for them, and re-layouts: 34 us -> 9.77 us
  Pallas kernels: 43.8 us -> 56.1 us
  other arithmetic: 5.12 us -> 2.56 us
  starting transfers between devices: 17.6 us -> 15.4 us
    unnamed x68 -> x23, local copies, waits for them, and re-layouts: 26.2 us -> 3.59 us
    ppermute x4 -> x3, starting transfers between devices: 14.9 us -> 10.3 us  [shifted(): return lax.ppermute(shard, axis, pairs)]
    pallas_call x2, Pallas kernels: 8.75 us -> 12.6 us  [conv_half(): pl.pallas_call(functools.partial(conv_kernel, taps=taps), grid_spec=pltpu...]
    pallas_call x1, Pallas kernels: 11.2 us -> 14.3 us  [local(): pl.pallas_call(body, grid_spec=pltpu.PrefetchScalarGridSpec(num_scalar_pr...]
    pallas_call x1, Pallas kernels: 6.61 us -> 9.57 us  [local(): pl.pallas_call(product_kernel, grid_spec=pltpu.PrefetchScalarGridSpec(num...]
    ppermute x6, starting transfers between devices: 2.7 us -> 5.07 us  [swapped(): lax.ppermute(shard, axis, [(i, i ^ 1) for i in range(lax.axis_size(axis))])]
    convert_element_type x1, other arithmetic: 2.01 us -> 0.16 us  [local(): leaving = (state.astype(F32) + kept[:1] * arriving.astype(F32)).astype(BF16)]
    dynamic_slice x2 -> x0, local copies, waits for them, and re-layouts: 1.47 us -> none  [the longest x1 1.39 us: local(): lax.dynamic_slice_in_dim(step_raw, (1 - sub) * heads, heads, 1)]
  transfers between devices with their start and end apart: 10 -> 9, of which waited for: 3 -> 3; matrix products, arithmetic and copies ran while one was open for 10% -> 5% of each run, Pallas kernels for 16% -> 24%
where the time goes in v1:
time: 119 us; the launch traced here: 118 us
  Pallas kernels  56.1 us (47%)
  waiting for transfers between devices  34.5 us (29%)
  starting transfers between devices  15.4 us (13%)
  local copies, waits for them, and re-layouts  9.77 us (8%)
  other arithmetic  2.56 us (2%)
    ppermute x6, waiting for transfers between devices, swapped(): lax.ppermute(shard, axis, [(i, i ^ 1) for i in range(lax.axis_size(axis))])  23.6 us
    pallas_call x1, Pallas kernels, local(): pl.pallas_call(body, grid_spec=pltpu.PrefetchScalarGridSpec(num_scalar_pr...  14.3 us
    pallas_call x1, Pallas kernels, local(): pl.pallas_call(functools.partial(intra_kernel, head_width=head_width, gro...  12.8 us
    pallas_call x2, Pallas kernels, conv_half(): pl.pallas_call(functools.partial(conv_kernel, taps=taps), grid_spec=pltpu...  12.6 us
    ppermute x3, waiting for transfers between devices, shifted(): return lax.ppermute(shard, axis, pairs)  10.9 us
    ppermute x3, starting transfers between devices, shifted(): return lax.ppermute(shard, axis, pairs)  10.3 us
    pallas_call x1, Pallas kernels, local(): pl.pallas_call(product_kernel, grid_spec=pltpu.PrefetchScalarGridSpec(num...  9.57 us
    pallas_call x1, Pallas kernels, local(): pl.pallas_call(functools.partial(state_kernel, head_width=head_width, gro...  6.72 us
  transfers between devices with their start and end apart: 9, of which 3 were waited for; matrix products, arithmetic and copies ran while one was open for 5% of the time, Pallas kernels for 24%

profile of v1, /device:TPU:0, one launch (start us, length us, event | category | flops | bytes accessed | tf_op | source)
XLA Modules:
  0.0 118.4 jit_solution(17120935454161671030)
XLA Ops:
  0.0 0.8 slice.13
  0.8 0.9 slice.12
  1.8 2.4 %collective-permute-start = (bf16[16,5120]{1,0:T(8,128)(2,1)S(1)}, bf16[16,5120]{1,0:T(8,128)(2,1)S(1)}, u32[]{:S(2)}, u32[]{:S(2)}) collective-permute-start(bf16[16,5120]{1,0:T(8,128)(2,1)S(1)} %pad_maximum_fusion), channel_id=1, source_target_pairs={{0,1},{1,4},{4,5},{5,8},{8,9},{9,12},{12,13},{2,3},{3,6},{6,7},{7,... | collective-permute-start | bytes 491528 | tf_op jit(solution)/shard_map/ppermute | solution.py:24
  4.1 2.2 %reshape.23.s = bf16[256,1024]{1,0:T(8,128)(2,1)} reshape(bf16[256,4,2,128]{3,2,1,0:T(2,128)(2,1)} %param.15) | data formatting | bytes 1048576 | tf_op jit(solution)/shard_map/reshape | solution.py:340
  6.3 1.3 %reshape.24.sw = bf16[4,1024]{1,0:T(4,128)(2,1)} reshape(bf16[4,4,2,128]{3,2,1,0:T(2,128)(2,1)} %param.18) | data formatting | bytes 16384 | tf_op jit(solution)/shard_map/reshape | solution.py:341
  7.6 0.7 pad_add_fusion.meta.m
  8.3 0.7 copy-done.2
  9.0 6.4 %conv.3 = bf16[256,2560]{1,0:T(8,128)(2,1)} custom-call(s32[3]{0:T(128)} %pad_add_fusion.meta.m, s32[8]{0:T(128)} %docs.7, bf16[256,4096]{1,0:T(8,128)(2,1)} %x.3, bf16[16,5120]{1,0:T(8,128)(2,1)} %copy-done.2, bf16[4,4096]{1,0:T(4,128)(2,1)} %w.4, f32[1,4096]{1,0:T(1,128)} %bitcast.9, bf16[256,1024]{1,0:T(8,128)(2,1)} %reshape.23.s, ...), custom_call_target="tpu_custom_call" | custom-call | flops 4194304 | bytes 2621440 | tf_op jit(solution)/shard_map/conv/pallas_call | solution.py:134
  15.4 2.7 %collective-permute-start.1 = (bf16[256,2560]{1,0:T(8,128)(2,1)}, bf16[256,2560]{1,0:T(8,128)(2,1)S(1)}, u32[]{:S(2)}, u32[]{:S(2)}) collective-permute-start(bf16[256,2560]{1,0:T(8,128)(2,1)} %conv.3), channel_id=1, source_target_pairs={{0,1},{1,0},{2,3},{3,2},{4,5},{5,4},{6,7},{7,6},{8,9},{9,8},{10,11... | collective-permute-start | bytes 3932168 | tf_op jit(solution)/shard_map/ppermute | solution.py:28
  18.0 0.1 copy.15.own_raw
  18.2 6.3 %conv.2.own.own_bc = bf16[256,2560]{1,0:T(8,128)(2,1)} custom-call(s32[3]{0:T(128)} %pad_add_fusion.meta.m, s32[8]{0:T(128)} %docs.7, bf16[256,4096]{1,0:T(8,128)(2,1)} %x.3, bf16[16,5120]{1,0:T(8,128)(2,1)} %copy-done.2, bf16[4,4096]{1,0:T(4,128)(2,1)} %w.4, f32[1,4096]{1,0:T(1,128)} %bitcast.10, bf16[256,1024]{1,0:T(8,128)(2,1)} %reshape.23.s, ...), custom_call_target="tpu_custom_call" | custom-call | flops 4194304 | bytes 2621440 | tf_op jit(solution)/shard_map/conv/pallas_call | solution.py:134
  24.5 0.6 copy-done.9
  25.1 0.5 copy-done
  25.6 6.7 %state.1 = (bf16[512,2048]{1,0:T(8,128)(2,1)}, bf16[512,512]{1,0:T(8,128)(2,1)}, bf16[128,2048]{1,0:T(8,128)(2,1)}, f32[8,2048]{1,0:T(8,128)}, f32[512,32]{1,0:T(8,128)}, /*index=5*/f32[32,512]{1,0:T(8,128)}) custom-call(s32[3]{0:T(128)} %pad_add_fusion.meta.m, s32[8]{0:T(128)} %docs.7, bf16[256,2560]{1,0:T(8,128)(2,1)} %conv.2.own.own_bc, ...), custom_call_target="tpu_custom_call" | custom-call | flops 536870912 | bytes 5242880 | tf_op jit(solution)/shard_map/state/pallas_call | solution.py:359
  32.3 3.7 %collective-permute-start.4 = (bf16[128,2048]{1,0:T(8,128)(2,1)}, bf16[128,2048]{1,0:T(8,128)(2,1)S(1)}, u32[]{:S(2)}, u32[]{:S(2)}) collective-permute-start(bf16[128,2048]{1,0:T(8,128)(2,1)} %get-tuple-element.24), channel_id=1, source_target_pairs={{0,4},{4,8},{8,12},{1,5},{5,9},{9,13},{2,6},{6,10},{10,14},{3,7},{... | collective-permute-start | bytes 1572872 | tf_op jit(solution)/shard_map/ppermute | solution.py:24
  36.0 0.1 constant_dynamic-slice_fusion
  36.1 0.3 collective-permute-start.3
  36.4 0.8 slice.15
  37.2 10.9 %collective-permute-done.4 = bf16[128,2048]{1,0:T(8,128)(2,1)S(1)} collective-permute-done((bf16[128,2048]{1,0:T(8,128)(2,1)}, bf16[128,2048]{1,0:T(8,128)(2,1)S(1)}, u32[]{:S(2)}, u32[]{:S(2)}) %collective-permute-start.4) | collective-permute-done | bytes 524320 | tf_op jit(solution)/shard_map/ppermute | solution.py:24
  48.1 0.2 add_convert_fusion.2
  48.2 4.3 %collective-permute-start.5 = (bf16[128,2048]{1,0:T(8,128)(2,1)S(1)}, bf16[128,2048]{1,0:T(8,128)(2,1)S(1)}, u32[]{:S(2)}, u32[]{:S(2)}) collective-permute-start(bf16[128,2048]{1,0:T(8,128)(2,1)S(1)} %add_convert_fusion.2), channel_id=1, source_target_pairs={{0,4},{4,8},{8,12},{1,5},{5,9},{9,13},{2,6},{6,10},{10,14},{3,7},{... | collective-permute-start | bytes 1572872 | tf_op jit(solution)/shard_map/ppermute | solution.py:24
  52.6 1.0 copy-done.5
  53.6 12.8 %intra.1 = (f32[512,2048]{1,0:T(8,128)}, f32[512,2048]{1,0:T(8,128)}) custom-call(s32[3]{0:T(128)} %pad_add_fusion.meta.m, s32[8]{0:T(128)} %docs.7, bf16[512,2048]{1,0:T(8,128)(2,1)} %get-tuple-element.18.x, bf16[512,512]{1,0:T(8,128)(2,1)} %get-tuple-element.19.bc.b, f32[512,32]{1,0:T(8,128)} %get-tuple-element.20.cum, f32[32,512]{1,0:T(8,128)} %get-tuple-element.21.dlt, ...), custom_call_target="tpu_custom_call" | custom-call | flops 1073741824 | bytes 14680064 | tf_op jit(solution)/shard_map/intra/pallas_call | solution.py:409
  66.4 0.8 copy-done.7
  67.2 14.3 %project.1 = (bf16[512,2048]{1,0:T(8,128)(2,1)}, bf16[256,2048]{1,0:T(8,128)(2,1)}, f32[256,2048]{1,0:T(8,128)}) custom-call(s32[3]{0:T(128)} %pad_add_fusion.meta.m, f32[512,2048]{1,0:T(8,128)} %get-tuple-element.22.a, f32[512,2048]{1,0:T(8,128)} %get-tuple-element.23.f, bf16[512,512]{1,0:T(8,128)(2,1)} %get-tuple-element.19.bc.b, ...), custom_call_target="tpu_custom_call" | custom-call | flops 4294967296 | bytes 18874368 | tf_op jit(solution)/shard_map/project/pallas_call | solution.py:482
  81.5 9.6 %product.1 = (bf16[256,2048]{1,0:T(8,128)(2,1)}, f32[256,2048]{1,0:T(8,128)}) custom-call(s32[3]{0:T(128)} %pad_add_fusion.meta.m, bf16[512,2048]{1,0:T(8,128)(2,1)} %get-tuple-element.26.hidden, bf16[2048,4096]{1,0:T(8,128)(2,1)} %w.5), custom_call_target="tpu_custom_call" | custom-call | flops 4294967296 | bytes 10485760 | tf_op jit(solution)/shard_map/product/pallas_call | solution.py:511
  91.1 0.5 collective-permute-start.6
  91.6 0.3 add_convert_fusion.1
  91.8 1.5 %collective-permute-start.8 = (bf16[256,2048]{1,0:T(8,128)(2,1)S(1)}, bf16[256,2048]{1,0:T(8,128)(2,1)S(1)}, u32[]{:S(2)}, u32[]{:S(2)}) collective-permute-start(bf16[256,2048]{1,0:T(8,128)(2,1)S(1)} %add_convert_fusion.1), channel_id=1, source_target_pairs={{0,2},{2,0},{1,3},{3,1},{4,6},{6,4},{5,7},{7,5},{8,10},{10,8},{9,1... | collective-permute-start | bytes 3145736 | tf_op jit(solution)/shard_map/ppermute | solution.py:28
  93.4 0.7 collective-permute-done.6
  94.0 22.9 %collective-permute-done.8 = bf16[256,2048]{1,0:T(8,128)(2,1)S(1)} collective-permute-done((bf16[256,2048]{1,0:T(8,128)(2,1)S(1)}, bf16[256,2048]{1,0:T(8,128)(2,1)S(1)}, u32[]{:S(2)}, u32[]{:S(2)}) %collective-permute-start.8) | collective-permute-done | bytes 1048608 | tf_op jit(solution)/shard_map/ppermute | solution.py:28
  117.0 1.5 %add_convert_fusion = bf16[256,2048]{1,0:T(8,128)(2,1)} fusion(bf16[256,2048]{1,0:T(8,128)(2,1)S(1)} %collective-permute-done.8, f32[256,2048]{1,0:T(8,128)S(1)} %copy-done.3, bf16[256,2048]{1,0:T(8,128)(2,1)S(1)} %collective-permute-done.6), kind=kLoop, calls=%fused_computation | loop fusion | flops 2621440 | bytes 5242880 | tf_op jit(solution)/shard_map/convert_element_type | solution.py:537
  (27 shorter events, 0.2 us)
Async XLA Ops:
  1.8 6.5 %collective-permute-start = (bf16[16,5120]{1,0:T(8,128)(2,1)S(1)}, bf16[16,5120]{1,0:T(8,128)(2,1)S(1)}, u32[]{:S(2)}, u32[]{:S(2)}) collective-permute-start(bf16[16,5120]{1,0:T(8,128)(2,1)S(1)} %pad_maximum_fusion), channel_id=1, source_target_pairs={{0,1},{1,4},{4,5},{5,8},{8,9},{9,12},{12,13},{2,3},{3,6},{6,7},{7,... | collective-permute-start | bytes 491528 | tf_op jit(solution)/shard_map/ppermute | solution.py:24
  8.3 0.7 copy-start.2
  9.0 9.1 %copy-start.10 = (f32[256,64]{0,1:T(8,128)S(1)}, f32[256,64]{0,1:T(8,128)}, u32[]{:S(2)}) copy-start(f32[256,64]{0,1:T(8,128)} %param.20) | copy-start | bytes 196612
  15.4 9.1 %collective-permute-start.1 = (bf16[256,2560]{1,0:T(8,128)(2,1)}, bf16[256,2560]{1,0:T(8,128)(2,1)S(1)}, u32[]{:S(2)}, u32[]{:S(2)}) collective-permute-start(bf16[256,2560]{1,0:T(8,128)(2,1)} %conv.3), channel_id=1, source_target_pairs={{0,1},{1,0},{2,3},{3,2},{4,5},{5,4},{6,7},{7,6},{8,9},{9,8},{10,11... | collective-permute-start | bytes 3932168 | tf_op jit(solution)/shard_map/ppermute | solution.py:28
  18.1 6.3 %copy-start.8 = (f32[256,64]{1,0:T(8,128)}, f32[256,64]{1,0:T(8,128)S(1)}, u32[]{:S(2)}) copy-start(f32[256,64]{1,0:T(8,128)S(1)} %copy.15.own_raw) | copy-start | bytes 196612
  18.1 6.3 %collective-permute-start.2 = (f32[256,64]{1,0:T(8,128)S(1)}, f32[256,64]{1,0:T(8,128)S(1)}, u32[]{:S(2)}, u32[]{:S(2)}) collective-permute-start(f32[256,64]{1,0:T(8,128)S(1)} %copy.15.own_raw), channel_id=1, source_target_pairs={{0,1},{1,0},{2,3},{3,2},{4,5},{5,4},{6,7},{7,6},{8,9},{9,8},{10,11... | collective-permute-start | bytes 196616 | tf_op jit(solution)/shard_map/ppermute | solution.py:28
  24.5 0.6 copy-start.9
  24.5 1.1 copy-start
  25.6 10.4 %copy-start.1 = (bf16[256,4096]{1,0:T(8,128)(2,1)S(1)}, bf16[256,4096]{1,0:T(8,128)(2,1)}, u32[]{:S(2)}) copy-start(bf16[256,4096]{1,0:T(8,128)(2,1)} %gate_own.1) | copy-start | bytes 6291460
  32.3 15.8 %copy-start.6 = (bf16[128,2048]{1,0:T(8,128)(2,1)S(1)}, bf16[128,2048]{1,0:T(8,128)(2,1)}, u32[]{:S(2)}) copy-start(bf16[128,2048]{1,0:T(8,128)(2,1)} %get-tuple-element.24) | copy-start | bytes 1572868
  32.3 15.8 %collective-permute-start.4 = (bf16[128,2048]{1,0:T(8,128)(2,1)}, bf16[128,2048]{1,0:T(8,128)(2,1)S(1)}, u32[]{:S(2)}, u32[]{:S(2)}) collective-permute-start(bf16[128,2048]{1,0:T(8,128)(2,1)} %get-tuple-element.24), channel_id=1, source_target_pairs={{0,4},{4,8},{8,12},{1,5},{5,9},{9,13},{2,6},{6,10},{10,14},{3,7},{... | collective-permute-start | bytes 1572872 | tf_op jit(solution)/shard_map/ppermute | solution.py:24
  36.1 16.5 %collective-permute-start.3 = (bf16[256,2048]{1,0:T(8,128)(2,1)S(1)}, bf16[256,2048]{1,0:T(8,128)(2,1)S(1)}, u32[]{:S(2)}, u32[]{:S(2)}) collective-permute-start(bf16[256,2048]{1,0:T(8,128)(2,1)S(1)} %constant_dynamic-slice_fusion), channel_id=1, source_target_pairs={{0,1},{1,0},{2,3},{3,2},{4,5},{5,4},{6,7},{7,6},{8,9},{9,8},{10,11... | collective-permute-start | bytes 3145736 | tf_op jit(solution)/shard_map/ppermute | solution.py:28
  48.2 18.1 %collective-permute-start.5 = (bf16[128,2048]{1,0:T(8,128)(2,1)S(1)}, bf16[128,2048]{1,0:T(8,128)(2,1)S(1)}, u32[]{:S(2)}, u32[]{:S(2)}) collective-permute-start(bf16[128,2048]{1,0:T(8,128)(2,1)S(1)} %add_convert_fusion.2), channel_id=1, source_target_pairs={{0,4},{4,8},{8,12},{1,5},{5,9},{9,13},{2,6},{6,10},{10,14},{3,7},{... | collective-permute-start | bytes 1572872 | tf_op jit(solution)/shard_map/ppermute | solution.py:24
  52.6 1.0 copy-start.5
  66.4 0.8 copy-start.7
  81.5 10.1 %collective-permute-start.7 = (bf16[256,2048]{1,0:T(8,128)(2,1)}, bf16[256,2048]{1,0:T(8,128)(2,1)S(1)}, u32[]{:S(2)}, u32[]{:S(2)}) collective-permute-start(bf16[256,2048]{1,0:T(8,128)(2,1)} %get-tuple-element.30), channel_id=1, source_target_pairs={{0,1},{1,0},{2,3},{3,2},{4,5},{5,4},{6,7},{7,6},{8,9},{9,8},{10,11... | collective-permute-start | bytes 3145736 | tf_op jit(solution)/shard_map/ppermute | solution.py:28
  81.5 10.1 %copy-start.4 = (f32[256,2048]{1,0:T(8,128)S(1)}, f32[256,2048]{1,0:T(8,128)}, u32[]{:S(2)}) copy-start(f32[256,2048]{1,0:T(8,128)} %get-tuple-element.29) | copy-start | bytes 6291460
  91.1 3.0 %collective-permute-start.6 = (bf16[256,2048]{1,0:T(8,128)(2,1)}, bf16[256,2048]{1,0:T(8,128)(2,1)S(1)}, u32[]{:S(2)}, u32[]{:S(2)}) collective-permute-start(bf16[256,2048]{1,0:T(8,128)(2,1)} %get-tuple-element.28), channel_id=1, source_target_pairs={{0,1},{1,0},{2,3},{3,2},{4,5},{5,4},{6,7},{7,6},{8,9},{9,8},{10,11... | collective-permute-start | bytes 3145736 | tf_op jit(solution)/shard_map/ppermute | solution.py:28
  91.6 25.4 %copy-start.3 = (f32[256,2048]{1,0:T(8,128)S(1)}, f32[256,2048]{1,0:T(8,128)}, u32[]{:S(2)}) copy-start(f32[256,2048]{1,0:T(8,128)} %get-tuple-element.27) | copy-start | bytes 6291460
  91.8 25.2 %collective-permute-start.8 = (bf16[256,2048]{1,0:T(8,128)(2,1)S(1)}, bf16[256,2048]{1,0:T(8,128)(2,1)S(1)}, u32[]{:S(2)}, u32[]{:S(2)}) collective-permute-start(bf16[256,2048]{1,0:T(8,128)(2,1)S(1)} %add_convert_fusion.1), channel_id=1, source_target_pairs={{0,2},{2,0},{1,3},{3,1},{4,6},{6,4},{5,7},{7,5},{8,10},{10,8},{9,1... | collective-permute-start | bytes 3145736 | tf_op jit(solution)/shard_map/ppermute | solution.py:28
